TPU v7x, 32 devices: a whole 2x2x4 slice. The times are simulated.
32 devices in a mesh: sub: 4 (over z), grp: 8 (over y, x, core).
Axes of the slice: x: 2, y: 2, z: 4, core: 2. Of those that a mesh axis runs over, the one named last changes fastest.
Arguments:
- schur: bfloat16 [128, 1024, 1024], P(('sub', 'grp')), as said below
- mortar: bfloat16 [128, 8, 128, 128], P(('sub', 'grp')), may hold values from -0.5 to 0.5
- partner: int32 [128, 4], P(('sub', 'grp')), may hold values from 0 to 15, as said below
- corner_map: int32 [128, 8], P(('sub', 'grp')), may hold values from 0 to 127
- coarse_inv: float32 [4, 128, 128], P('sub'), as said below
- load: float32 [128, 1024, 384], P(('sub', 'grp')), may hold values from -6 to 6
Outputs:
- solution: float32 [128, 1024, 384], P(('sub', 'grp'))
Inputs may be any that keep to these rules, and one draw needn't show every extreme that they name: `partner`: within the 4 subdomains of one device, the entries form a permutation of 0 to 15. `schur`: each matrix is symmetric positive definite. `coarse_inv`: each matrix is symmetric positive definite.
All inputs are finite; a program needn't handle non-finite values.
Results may differ from a plain program's by a relative error of at most 0.0025.
Values may be sent and summed in bfloat16 or wider, within the bound.
No kernel may reach another device: no remote copies, remote signals or barrier semaphores. Data moves between devices by JAX's collectives and lax.ppermute only.
A program may use at most 128 MiB of HBM per device.

v0:
```python
import jax
import jax.numpy as jnp
from jax import lax
from jax.sharding import PartitionSpec as P

ITERS = 2


def shifted(block, axis, distance):
    devices = range(lax.axis_size(axis))
    route = [((i - distance) % len(devices), i) for i in devices]
    return lax.ppermute(block, axis, route)


def face_terms(direction, schur, mortar, partner):
    subdoms = direction.shape[0]
    order = direction.shape[1]
    columns = direction.shape[2]
    faces_all = mortar.shape[1]
    block = mortar.shape[2]
    half_faces = faces_all // 2
    dir_half = direction.astype(jnp.bfloat16)
    stiff = jnp.einsum("sij,sjr->sir", schur, dir_half, preferred_element_type=jnp.float32)
    face_rows = dir_half.reshape(subdoms, faces_all, block, columns)
    traces = jnp.einsum(
        "sfij,sfjr->sfir", mortar, face_rows, preferred_element_type=jnp.float32
    ).astype(jnp.bfloat16)
    upper = traces[:, :half_faces].reshape(subdoms * half_faces, block, columns)
    lower = traces[:, half_faces:].reshape(subdoms * half_faces, block, columns)
    mates = partner.reshape(-1)
    inverse = jnp.argsort(mates)
    reordered = jnp.take(upper, inverse, axis=0)
    lower_mate = shifted(reordered, "sub", 1)
    jump_lower = (lower.astype(jnp.float32) - lower_mate.astype(jnp.float32)).astype(jnp.bfloat16)
    above = shifted(lower, "sub", -1)
    upper_mate = jnp.take(above, mates, axis=0)
    jump_upper = (upper.astype(jnp.float32) - upper_mate.astype(jnp.float32)).astype(jnp.bfloat16)
    jump_all = jnp.concatenate(
        [
            jump_upper.reshape(subdoms, half_faces, block, columns),
            jump_lower.reshape(subdoms, half_faces, block, columns),
        ],
        axis=1,
    )
    pulled = jnp.einsum("sfji,sfjr->sfir", mortar, jump_all, preferred_element_type=jnp.float32)
    return stiff + pulled.reshape(subdoms, order, columns)


def squares(residual):
    return lax.psum(jnp.sum(residual * residual, axis=(0, 1)), ("sub", "grp"))


def on_device(schur, mortar, partner, corner_map, coarse_inv, load):
    order = load.shape[1]
    corner_count = corner_map.shape[1]
    coarse_count = coarse_inv.shape[1]
    stride = order // corner_count
    onehot = (corner_map[..., None] == jnp.arange(coarse_count, dtype=jnp.int32)).astype(
        jnp.float32
    )
    coarse_matrix = coarse_inv[0]
    solution = jnp.zeros_like(load)
    residual = load
    direction = load
    norm_now = squares(residual)
    for step in range(ITERS):
        partial_value = face_terms(direction, schur, mortar, partner)
        corners = direction[:, ::stride, :]
        local_sum = jnp.einsum("sco,scr->or", onehot, corners, precision=lax.Precision.HIGHEST)
        local_dot = jnp.sum(direction * partial_value, axis=(0, 1))
        coarse_sum = lax.psum(local_sum.astype(jnp.bfloat16), "grp").astype(jnp.float32)
        group_dot = lax.psum(local_dot.astype(jnp.bfloat16), "grp").astype(jnp.float32)
        coarse_val = jnp.dot(coarse_matrix, coarse_sum, precision=lax.Precision.HIGHEST)
        corner_add = jnp.einsum("sco,or->scr", onehot, coarse_val, precision=lax.Precision.HIGHEST)
        image = partial_value.at[:, ::stride, :].add(corner_add)
        curvature = lax.psum(group_dot + jnp.sum(coarse_sum * coarse_val, axis=0), "sub")
        image, curvature = (image, curvature)
        step_len = norm_now / curvature
        solution = solution + step_len * direction
        if step + 1 < ITERS:
            residual = residual - step_len * image
            norm_next = squares(residual)
            direction = residual + norm_next / norm_now * direction
            norm_now = norm_next
    return solution


def solution(mesh):
    return jax.shard_map(
        on_device,
        mesh=mesh,
        in_specs=(
            P(("sub", "grp"), None, None),
            P(("sub", "grp"), None, None, None),
            P(("sub", "grp"), None),
            P(("sub", "grp"), None),
            P("sub", None, None),
            P(("sub", "grp"), None, None),
        ),
        out_specs=P(("sub", "grp"), None, None),
        check_vma=False,
    )
```

profile of v0, /device:TPU:0, one launch (start us, length us, event | category | flops | bytes accessed | tf_op | source)
XLA Modules:
  0.0 398.2 jit_solution(7781319759656753900)
XLA Ops:
  12.3 5.1 %collective-permute-start = (bf16[16,128,384]{2,1,0:T(8,128)(2,1)}, bf16[16,128,384]{2,1,0:T(8,128)(2,1)}, u32[]{:S(2)}, u32[]{:S(2)}) collective-permute-start(bf16[16,128,384]{2,1,0:T(8,128)(2,1)} %bitcast.2), channel_id=1, source_target_pairs={{8,0},{16,8},{24,16},{0,24},{9,1},{17,9},{25,17},{1,25},{10,2},{18... | collective-permute-start | bytes 4718600 | tf_op jit(solution)/shard_map/ppermute | solution.py:12
  27.4 6.6 %copy.8 = f32[4,1024,384]{1,2,0:T(8,128)} copy(f32[4,1024,384]{2,1,0:T(8,128)} %param.13) | data formatting | bytes 12582912 | tf_op args[5]
  34.0 46.9 %all-reduce.3.cloned.1.call-done = bf16[128,384]{1,0:T(8,128)(2,1)} async-done(((bf16[128,384]{1,0:T(8,128)(2,1)}), bf16[128,384]{1,0:T(8,128)(2,1)}) %all-reduce.3.cloned.1.call-update) | async-done | bytes 98320 | tf_op jit(solution)/shard_map/psum | solution.py:71
  90.4 3.7 fusion.5
  94.1 12.9 %multiply_reduce_fusion.1 = (bf16[384]{0:T(512)(128)(2,1)S(1)}, f32[384]{0:T(512)S(1)}, f32[4,1024,384]{2,1,0:T(8,128)}) fusion(f32[4,1024,384]{2,1,0:T(8,128)S(1)} %bitcast.79, f32[4,8,384,128]{2,3,1,0:T(8,128)} %fusion.5, bf16[4,1024,1024]{2,1,0:T(8,128)(2,1)} %param.8), kind=kOutput, calls=%fused_computation.13 | convolution fusion | flops 3230661632 | bytes 27265280 | tf_op jit(solution)/shard_map/sij,sjr->sir/dot_general | solution.py:23
  107.0 12.8 %psum.57 = bf16[384]{0:T(512)(128)(2,1)S(1)} all-reduce(bf16[384]{0:T(512)(128)(2,1)S(1)} %get-tuple-element.8), channel_id=1, replica_groups=mesh['sub'=4,'grp'=8] {'grp'}, use_global_device_ids=true, to_apply=%region_4.6 | all-reduce | flops 384 | bytes 1536 | tf_op jit(solution)/shard_map/psum | solution.py:72
  119.8 11.7 %psum.59 = f32[384]{0:T(512)S(1)} all-reduce(f32[384]{0:T(512)S(1)} %convert_add_fusion.1), channel_id=1, replica_groups=mesh['sub'=4,'grp'=8] {'sub'}, use_global_device_ids=true, to_apply=%region_7.9 | all-reduce | flops 384 | bytes 3072 | tf_op jit(solution)/shard_map/psum | solution.py:76
  131.5 37.0 %psum.56 = f32[384]{0:T(512)S(1)} all-reduce(f32[384]{0:T(512)S(1)} %get-tuple-element.9), channel_id=1, replica_groups=mesh['sub'=4,'grp'=8] {'sub','grp'}, use_global_device_ids=true, to_apply=%region_1.0 | all-reduce | flops 384 | bytes 3072 | tf_op jit(solution)/shard_map/psum | solution.py:50
  168.5 9.5 %copy.10 = f32[4,1024,384]{2,0,1:T(4,128)} copy(f32[4,1024,384]{2,1,0:T(8,128)} %get-tuple-element.16) | data formatting | bytes 12582912 | tf_op jit(solution)/shard_map/add | solution.py:46
  180.0 7.6 %copy.12 = f32[4,1024,384]{1,2,0:T(8,128)} copy(f32[4,1024,384]{2,0,1:T(4,128)} %scatter_fusion) | data formatting | bytes 12582912 | tf_op jit(solution)/shard_map/scatter-add | solution.py:75
  187.7 5.6 %multiply_reduce_fusion = f32[384]{0:T(512)S(1)} fusion(f32[4,1024,384]{1,2,0:T(8,128)} %copy.8, f32[4,1024,384]{1,2,0:T(8,128)} %copy.12, f32[384]{0:T(512)S(1)} %div.9), kind=kLoop, calls=%fused_computation.11 | loop fusion | flops 6291072 | bytes 12585984 | tf_op jit(solution)/shard_map/reduce_sum | solution.py:50
  193.3 42.2 %psum.60 = f32[384]{0:T(512)S(1)} all-reduce(f32[384]{0:T(512)S(1)} %multiply_reduce_fusion), channel_id=1, replica_groups=mesh['sub'=4,'grp'=8] {'sub','grp'}, use_global_device_ids=true, to_apply=%region_10.12 | all-reduce | flops 384 | bytes 3072 | tf_op jit(solution)/shard_map/psum | solution.py:50
  235.5 7.7 %convert_bitcast_fusion.1 = (bf16[4,48,8,8,128]{4,3,2,1,0:T(8,128)(2,1)S(1)}, f32[4,1024,384]{1,2,0:T(8,128)}) fusion(f32[4,1024,384]{1,2,0:T(8,128)} %copy.8, f32[384]{0:T(512)S(1)} %div.10, f32[4,1024,384]{1,2,0:T(8,128)} %copy.12, f32[384]{0:T(512)S(1)} %div.9), kind=kLoop, calls=%fused_computation.32 | loop fusion | flops 7864320 | bytes 22023168
  252.3 4.3 %slice.23 = f32[4,8,384]{1,2,0:T(8,128)S(1)} slice(f32[4,1024,384]{1,2,0:T(8,128)} %get-tuple-element.11), slice={[0:4:1], [0:1024:128], [0:384:1]} | slice | bytes 98304 | tf_op jit(solution)/shard_map/slice | solution.py:68
  257.9 53.1 %all-reduce.5.cloned.1.call-done = bf16[128,384]{1,0:T(8,128)(2,1)} async-done(((bf16[128,384]{1,0:T(8,128)(2,1)}), bf16[128,384]{1,0:T(8,128)(2,1)}) %all-reduce.5.cloned.1.call-update) | async-done | bytes 98320 | tf_op jit(solution)/shard_map/psum | solution.py:71
  314.9 3.3 gather_fusion.2
  323.3 3.4 subtract_convert_fusion
  329.3 5.1 %fusion.9 = f32[4,8,384,128]{2,3,1,0:T(8,128)} fusion(bf16[4,8,128,128]{3,2,1,0:T(8,128)(2,1)S(1)} %copy-done, bf16[4,4,128,384]{3,2,1,0:T(8,128)(2,1)} %bitcast.87, bf16[4,4,128,384]{3,2,1,0:T(8,128)(2,1)S(1)} %bitcast.85), kind=kOutput, calls=%fused_computation.22 | convolution fusion | flops 404226048 | bytes 10485760 | tf_op jit(solution)/shard_map/sfji,sfjr->sfir/dot_general | solution.py:45
  334.4 6.5 %copy.27 = f32[4,1024,384]{1,2,0:T(8,128)} copy(f32[4,1024,384]{2,1,0:T(8,128)} %bitcast.80) | data formatting | bytes 12582912 | tf_op jit(solution)/shard_map/reshape | solution.py:46
  340.9 12.5 %fusion.1 = bf16[384]{0:T(512)(128)(2,1)S(1)} fusion(f32[4,1024,384]{1,2,0:T(8,128)} %get-tuple-element.11, f32[4,1024,384]{1,2,0:T(8,128)} %copy.27, bf16[4,1024,1024]{2,1,0:T(8,128)(2,1)} %param.8), kind=kOutput, calls=%fused_computation.8 | convolution fusion | flops 3227516416 | bytes 20972288 | tf_op jit(solution)/shard_map/sij,sjr->sir/dot_general | solution.py:23
  353.5 11.8 %psum.61 = bf16[384]{0:T(512)(128)(2,1)S(1)} all-reduce(bf16[384]{0:T(512)(128)(2,1)S(1)} %fusion.1), channel_id=1, replica_groups=mesh['sub'=4,'grp'=8] {'grp'}, use_global_device_ids=true, to_apply=%region_12.14 | all-reduce | flops 384 | bytes 1536 | tf_op jit(solution)/shard_map/psum | solution.py:72
  365.3 9.9 %psum.63 = f32[384]{0:T(512)S(1)} all-reduce(f32[384]{0:T(512)S(1)} %convert_add_fusion), channel_id=1, replica_groups=mesh['sub'=4,'grp'=8] {'sub'}, use_global_device_ids=true, to_apply=%region_15.17 | all-reduce | flops 384 | bytes 3072 | tf_op jit(solution)/shard_map/psum | solution.py:76
  375.2 9.6 %multiply_add_fusion = f32[4,1024,384]{1,2,0:T(8,128)} fusion(f32[4,1024,384]{1,2,0:T(8,128)} %get-tuple-element.11, f32[4,1024,384]{1,2,0:T(8,128)} %copy.8, f32[384]{0:T(512)S(1)} %div.11, f32[384]{0:T(512)S(1)} %div.9), kind=kLoop, calls=%fused_computation.9 | loop fusion | flops 4718592 | bytes 18877440 | tf_op jit(solution)/shard_map/add | solution.py:79
  384.8 6.6 %copy.21 = f32[4,1024,384]{2,1,0:T(8,128)} copy(f32[4,1024,384]{1,2,0:T(8,128)} %multiply_add_fusion) | data formatting | bytes 12582912 | tf_op jit(solution)/shard_map/add | solution.py:79
  (62 shorter events, 49.2 us)
Async XLA Ops:
  6.5 3.2 copy-start
  6.5 74.4 %all-reduce.3.cloned.1.call-start = ((), (), s32[]{:S(2)}) async-start(), calls=%async_computation | async-start | bytes 196608 | tf_op jit(solution)/shard_map/psum | solution.py:71
  10.8 6.6 %copy-start.3 = (s32[4,4]{1,0:T(4,128)S(1)}, s32[4,4]{1,0:T(4,128)}, u32[]{:S(2)}) copy-start(s32[4,4]{1,0:T(4,128)} %param.10) | copy-start | bytes 196
  12.3 70.1 %collective-permute-start = (bf16[16,128,384]{2,1,0:T(8,128)(2,1)}, bf16[16,128,384]{2,1,0:T(8,128)(2,1)}, u32[]{:S(2)}, u32[]{:S(2)}) collective-permute-start(bf16[16,128,384]{2,1,0:T(8,128)(2,1)} %bitcast.2), channel_id=1, source_target_pairs={{8,0},{16,8},{24,16},{0,24},{9,1},{17,9},{25,17},{1,25},{10,2},{18... | collective-permute-start | bytes 4718600 | tf_op jit(solution)/shard_map/ppermute | solution.py:12
  18.8 7.5 %copy-start.2 = (s32[4,8]{1,0:T(4,128)S(1)}, s32[4,8]{1,0:T(4,128)}, u32[]{:S(2)}) copy-start(s32[4,8]{1,0:T(4,128)} %param.11) | copy-start | bytes 388
  23.5 64.4 %collective-permute-start.1 = (bf16[16,128,384]{2,1,0:T(8,128)(2,1)}, bf16[16,128,384]{2,1,0:T(8,128)(2,1)}, u32[]{:S(2)}, u32[]{:S(2)}) collective-permute-start(bf16[16,128,384]{2,1,0:T(8,128)(2,1)} %broadcast_select_fusion.1), channel_id=1, source_target_pairs={{24,0},{0,8},{8,16},{16,24},{25,1},{1,9},{9,17},{17,25},{26,2},{2,... | collective-permute-start | bytes 4718600 | tf_op jit(solution)/shard_map/ppermute | solution.py:12
  27.3 283.6 %all-reduce.5.cloned.1.call-start = ((), (), s32[]{:S(2)}) async-start(), calls=%async_computation.1 | async-start | bytes 196608 | tf_op jit(solution)/shard_map/psum | solution.py:71
  27.4 53.5 %copy-start.1 = (f32[1,128,128]{2,1,0:T(8,128)S(1)}, f32[1,128,128]{2,1,0:T(8,128)}, u32[]{:S(2)}) copy-start(f32[1,128,128]{2,1,0:T(8,128)} %param.12) | copy-start | bytes 196612
  87.9 6.2 %slice-start = ((s8[6291456]{0:T(1024)(128)(4,1)}), s8[4194304]{0:T(1024)(128)(4,1)S(1)}, s32[]{:S(2)}) async-start(s8[6291456]{0:T(1024)(128)(4,1)} %bitcast.78), calls=%async_computation.2 | async-start | bytes 8388608
  90.4 3.7 slice-start.1
  245.6 69.3 %collective-permute-start.2 = (bf16[16,128,384]{1,2,0:T(8,128)(2,1)}, bf16[16,128,384]{1,2,0:T(8,128)(2,1)}, u32[]{:S(2)}, u32[]{:S(2)}) collective-permute-start(bf16[16,128,384]{1,2,0:T(8,128)(2,1)} %bitcast.16), channel_id=1, source_target_pairs={{8,0},{16,8},{24,16},{0,24},{9,1},{17,9},{25,17},{1,25},{10,2},{18... | collective-permute-start | bytes 4718600 | tf_op jit(solution)/shard_map/ppermute | solution.py:12
  251.8 71.5 %collective-permute-start.3 = (bf16[16,128,384]{1,2,0:T(8,128)(2,1)}, bf16[16,128,384]{1,2,0:T(8,128)(2,1)}, u32[]{:S(2)}, u32[]{:S(2)}) collective-permute-start(bf16[16,128,384]{1,2,0:T(8,128)(2,1)} %broadcast_select_fusion), channel_id=1, source_target_pairs={{24,0},{0,8},{8,16},{16,24},{25,1},{1,9},{9,17},{17,25},{26,2},{2,... | collective-permute-start | bytes 4718600 | tf_op jit(solution)/shard_map/ppermute | solution.py:12
Sparse Core Ops, SparseCore 0:
  27.4 53.4 all-reduce.2
  258.0 52.8 all-reduce.4
where the time goes:
time: 399 us; the launch traced here: 398 us
  blocking collectives  125 us (31%)
  waiting for transfers between devices  103 us (26%)
  local copies, waits for them, and re-layouts  61.9 us (16%)
  other arithmetic  46.2 us (12%)
  matrix products  41.1 us (10%)
  between operations  13.6 us (3%)
  starting transfers between devices  7.15 us (2%)
    psum x2, waiting for transfers between devices, on_device(): lax.psum(local_sum.astype(jnp.bfloat16), 'grp').astype(jnp.float32)  100 us
    psum x2, blocking collectives, squares(): return lax.psum(jnp.sum(residual * residual, axis=(0, 1)), ('sub', 'grp'))  79.2 us
    dot_general x2, matrix products, face_terms(): jnp.einsum('sij,sjr->sir', schur, dir_half, preferred_element_type=jnp.fl...  25.4 us
    psum x2, blocking collectives, on_device(): lax.psum(local_dot.astype(jnp.bfloat16), 'grp').astype(jnp.float32)  24.6 us
    psum x2, blocking collectives, on_device(): lax.psum(group_dot + jnp.sum(coarse_sum * coarse_val, axis=0), 'sub')  21.6 us
    add x1, other arithmetic, on_device(): solution = solution + step_len * direction  9.61 us
    add x1, local copies, waits for them, and re-layouts, face_terms(): return stiff + pulled.reshape(subdoms, order, columns)  9.48 us
    dot_general x2, matrix products, face_terms(): jnp.einsum('sfji,sfjr->sfir', mortar, jump_all, preferred_element_type=jn...  8.78 us
  transfers between devices with their start and end apart: 6, of which 3 were waited for; matrix products, arithmetic and copies ran while one was open for 11% of the time, Pallas kernels for 0%

commit v1 on v0

--- a/solution.py
+++ b/solution.py
@@ -47,7 +47,9 @@
 
 
 def squares(residual):
-    return lax.psum(jnp.sum(residual * residual, axis=(0, 1)), ("sub", "grp"))
+    return jnp.sum(
+        lax.all_gather(jnp.sum(residual * residual, axis=(0, 1)), ("sub", "grp")), axis=0
+    )
 
 
 def on_device(schur, mortar, partner, corner_map, coarse_inv, load):

time: 399 us -> 395 us (0.990)
  blocking collectives: 125 us -> 120 us
    psum x2 -> x0, blocking collectives: 79.2 us -> none  [squares(): return lax.psum(jnp.sum(residual * residual, axis=(0, 1)), ('sub', 'grp'))]
    all_gather x0 -> x2, blocking collectives: none -> 75.1 us  [squares(): lax.all_gather(jnp.sum(residual * residual, axis=(0, 1)), ('sub', 'grp'))]
    ppermute x4, waiting for transfers between devices: 2.79 us -> 7.37 us  [shifted(): return lax.ppermute(block, axis, route)]
where the time goes in v1:
time: 395 us; the launch traced here: 394 us
  blocking collectives  120 us (30%)
  waiting for transfers between devices  104 us (26%)
  local copies, waits for them, and re-layouts  61.9 us (16%)
  other arithmetic  46.4 us (12%)
  matrix products  41.1 us (10%)
  between operations  13.6 us (3%)
  starting transfers between devices  7.15 us (2%)
    psum x2, waiting for transfers between devices, on_device(): lax.psum(local_sum.astype(jnp.bfloat16), 'grp').astype(jnp.float32)  96.7 us
    all_gather x2, blocking collectives, squares(): lax.all_gather(jnp.sum(residual * residual, axis=(0, 1)), ('sub', 'grp'))  75.1 us
    dot_general x2, matrix products, face_terms(): jnp.einsum('sij,sjr->sir', schur, dir_half, preferred_element_type=jnp.fl...  25.4 us
    psum x2, blocking collectives, on_device(): lax.psum(local_dot.astype(jnp.bfloat16), 'grp').astype(jnp.float32)  24.6 us
    psum x2, blocking collectives, on_device(): lax.psum(group_dot + jnp.sum(coarse_sum * coarse_val, axis=0), 'sub')  20 us
    add x1, other arithmetic, on_device(): solution = solution + step_len * direction  9.61 us
    add x1, local copies, waits for them, and re-layouts, face_terms(): return stiff + pulled.reshape(subdoms, order, columns)  9.48 us
    dot_general x2, matrix products, face_terms(): jnp.einsum('sfji,sfjr->sfir', mortar, jump_all, preferred_element_type=jn...  8.78 us
  transfers between devices with their start and end apart: 6, of which 3 were waited for; matrix products, arithmetic and copies ran while one was open for 11% of the time, Pallas kernels for 0%

profile of v1, /device:TPU:0, one launch (start us, length us, event | category | flops | bytes accessed | tf_op | source)
XLA Modules:
  0.0 394.0 jit_solution(4392535690592030623)
XLA Ops:
  12.3 5.1 %collective-permute-start = (bf16[16,128,384]{2,1,0:T(8,128)(2,1)}, bf16[16,128,384]{2,1,0:T(8,128)(2,1)}, u32[]{:S(2)}, u32[]{:S(2)}) collective-permute-start(bf16[16,128,384]{2,1,0:T(8,128)(2,1)} %bitcast.2), channel_id=1, source_target_pairs={{8,0},{16,8},{24,16},{0,24},{9,1},{17,9},{25,17},{1,25},{10,2},{18... | collective-permute-start | bytes 4718600 | tf_op jit(solution)/shard_map/ppermute | solution.py:12
  27.4 6.6 %copy.23 = f32[4,1024,384]{1,2,0:T(8,128)} copy(f32[4,1024,384]{2,1,0:T(8,128)} %param.13) | data formatting | bytes 12582912 | tf_op args[5]
  34.0 46.9 %all-reduce.3.cloned.1.call-done = bf16[128,384]{1,0:T(8,128)(2,1)} async-done(((bf16[128,384]{1,0:T(8,128)(2,1)}), bf16[128,384]{1,0:T(8,128)(2,1)}) %all-reduce.3.cloned.1.call-update) | async-done | bytes 98320 | tf_op jit(solution)/shard_map/psum | solution.py:73
  90.4 3.7 fusion.5
  94.1 12.9 %multiply_reduce_fusion.1 = (bf16[384]{0:T(512)(128)(2,1)S(1)}, f32[384]{0:T(512)S(1)}, f32[4,1024,384]{2,1,0:T(8,128)}) fusion(f32[4,1024,384]{2,1,0:T(8,128)S(1)} %bitcast.79, f32[4,8,384,128]{2,3,1,0:T(8,128)} %fusion.5, bf16[4,1024,1024]{2,1,0:T(8,128)(2,1)} %param.8), kind=kOutput, calls=%fused_computation.13 | convolution fusion | flops 3230661632 | bytes 27265280 | tf_op jit(solution)/shard_map/sij,sjr->sir/dot_general | solution.py:23
  107.0 12.8 %psum.42 = bf16[384]{0:T(512)(128)(2,1)S(1)} all-reduce(bf16[384]{0:T(512)(128)(2,1)S(1)} %get-tuple-element.8), channel_id=1, replica_groups=mesh['sub'=4,'grp'=8] {'grp'}, use_global_device_ids=true, to_apply=%region_4.6 | all-reduce | flops 384 | bytes 1536 | tf_op jit(solution)/shard_map/psum | solution.py:74
  119.8 11.7 %psum.44 = f32[384]{0:T(512)S(1)} all-reduce(f32[384]{0:T(512)S(1)} %convert_add_fusion.1), channel_id=1, replica_groups=mesh['sub'=4,'grp'=8] {'sub'}, use_global_device_ids=true, to_apply=%region_7.9 | all-reduce | flops 384 | bytes 3072 | tf_op jit(solution)/shard_map/psum | solution.py:78
  131.5 36.6 %all-gather.2 = f32[32,1,384]{2,1,0:T(1,128)S(1)} all-gather(f32[1,1,384]{2,1,0:T(1,128)S(1)} %reshape.119), channel_id=2, replica_groups=mesh['sub'=4,'grp'=8] {'sub','grp'}, dimensions={0}, use_global_device_ids=true | all-gather | bytes 50688 | tf_op jit(solution)/shard_map/all_gather | solution.py:51
  168.1 9.5 %copy.25 = f32[4,1024,384]{2,0,1:T(4,128)} copy(f32[4,1024,384]{2,1,0:T(8,128)} %get-tuple-element.16) | data formatting | bytes 12582912 | tf_op jit(solution)/shard_map/add | solution.py:46
  179.7 7.6 %copy.27 = f32[4,1024,384]{1,2,0:T(8,128)} copy(f32[4,1024,384]{2,0,1:T(4,128)} %scatter_fusion) | data formatting | bytes 12582912 | tf_op jit(solution)/shard_map/scatter-add | solution.py:77
  187.4 5.6 %multiply_reduce_fusion = f32[384]{0:T(512)S(1)} fusion(f32[4,1024,384]{1,2,0:T(8,128)} %copy.23, f32[4,1024,384]{1,2,0:T(8,128)} %copy.27, f32[384]{0:T(512)S(1)} %div.13), kind=kLoop, calls=%fused_computation.11 | loop fusion | flops 6291072 | bytes 12585984 | tf_op jit(solution)/shard_map/reduce_sum | solution.py:51
  193.0 38.4 %all-gather.3 = f32[32,1,384]{2,1,0:T(1,128)S(1)} all-gather(f32[1,1,384]{2,1,0:T(1,128)S(1)} %reshape.121), channel_id=3, replica_groups=mesh['sub'=4,'grp'=8] {'sub','grp'}, dimensions={0}, use_global_device_ids=true | all-gather | bytes 50688 | tf_op jit(solution)/shard_map/all_gather | solution.py:51
  231.5 7.7 %convert_bitcast_fusion.1 = (bf16[4,48,8,8,128]{4,3,2,1,0:T(8,128)(2,1)S(1)}, f32[4,1024,384]{1,2,0:T(8,128)}) fusion(f32[4,1024,384]{1,2,0:T(8,128)} %copy.23, f32[384]{0:T(512)S(1)} %div.14, f32[4,1024,384]{1,2,0:T(8,128)} %copy.27, f32[384]{0:T(512)S(1)} %div.13), kind=kLoop, calls=%fused_computation.32 | loop fusion | flops 7864320 | bytes 22023168
  248.3 4.3 %slice.23 = f32[4,8,384]{1,2,0:T(8,128)S(1)} slice(f32[4,1024,384]{1,2,0:T(8,128)} %get-tuple-element.11), slice={[0:4:1], [0:1024:128], [0:384:1]} | slice | bytes 98304 | tf_op jit(solution)/shard_map/slice | solution.py:70
  253.9 49.8 %all-reduce.5.cloned.1.call-done = bf16[128,384]{1,0:T(8,128)(2,1)} async-done(((bf16[128,384]{1,0:T(8,128)(2,1)}), bf16[128,384]{1,0:T(8,128)(2,1)}) %all-reduce.5.cloned.1.call-update) | async-done | bytes 98320 | tf_op jit(solution)/shard_map/psum | solution.py:73
  304.9 7.4 %collective-permute-done.2 = bf16[16,128,384]{1,2,0:T(8,128)(2,1)} collective-permute-done((bf16[16,128,384]{1,2,0:T(8,128)(2,1)}, bf16[16,128,384]{1,2,0:T(8,128)(2,1)}, u32[]{:S(2)}, u32[]{:S(2)}) %collective-permute-start.2) | collective-permute-done | bytes 1572896 | tf_op jit(solution)/shard_map/ppermute | solution.py:12
  320.6 3.4 subtract_convert_fusion
  326.6 5.1 %fusion.9 = f32[4,8,384,128]{2,3,1,0:T(8,128)} fusion(bf16[4,8,128,128]{3,2,1,0:T(8,128)(2,1)S(1)} %copy-done, bf16[4,4,128,384]{3,2,1,0:T(8,128)(2,1)} %bitcast.87, bf16[4,4,128,384]{3,2,1,0:T(8,128)(2,1)S(1)} %bitcast.85), kind=kOutput, calls=%fused_computation.22 | convolution fusion | flops 404226048 | bytes 10485760 | tf_op jit(solution)/shard_map/sfji,sfjr->sfir/dot_general | solution.py:45
  331.7 6.5 %copy.42 = f32[4,1024,384]{1,2,0:T(8,128)} copy(f32[4,1024,384]{2,1,0:T(8,128)} %bitcast.80) | data formatting | bytes 12582912 | tf_op jit(solution)/shard_map/reshape | solution.py:46
  338.3 12.5 %fusion.1 = bf16[384]{0:T(512)(128)(2,1)S(1)} fusion(f32[4,1024,384]{1,2,0:T(8,128)} %get-tuple-element.11, f32[4,1024,384]{1,2,0:T(8,128)} %copy.42, bf16[4,1024,1024]{2,1,0:T(8,128)(2,1)} %param.8), kind=kOutput, calls=%fused_computation.8 | convolution fusion | flops 3227516416 | bytes 20972288 | tf_op jit(solution)/shard_map/sij,sjr->sir/dot_general | solution.py:23
  350.8 11.8 %psum.45 = bf16[384]{0:T(512)(128)(2,1)S(1)} all-reduce(bf16[384]{0:T(512)(128)(2,1)S(1)} %fusion.1), channel_id=1, replica_groups=mesh['sub'=4,'grp'=8] {'grp'}, use_global_device_ids=true, to_apply=%region_12.14 | all-reduce | flops 384 | bytes 1536 | tf_op jit(solution)/shard_map/psum | solution.py:74
  362.6 8.4 %psum.47 = f32[384]{0:T(512)S(1)} all-reduce(f32[384]{0:T(512)S(1)} %convert_add_fusion), channel_id=1, replica_groups=mesh['sub'=4,'grp'=8] {'sub'}, use_global_device_ids=true, to_apply=%region_15.17 | all-reduce | flops 384 | bytes 3072 | tf_op jit(solution)/shard_map/psum | solution.py:78
  371.0 9.6 %multiply_add_fusion = f32[4,1024,384]{1,2,0:T(8,128)} fusion(f32[4,1024,384]{1,2,0:T(8,128)} %get-tuple-element.11, f32[4,1024,384]{1,2,0:T(8,128)} %copy.23, f32[384]{0:T(512)S(1)} %div.15, f32[384]{0:T(512)S(1)} %div.13), kind=kLoop, calls=%fused_computation.9 | loop fusion | flops 4718592 | bytes 18877440 | tf_op jit(solution)/shard_map/add | solution.py:81
  380.6 6.6 %copy.36 = f32[4,1024,384]{2,1,0:T(8,128)} copy(f32[4,1024,384]{1,2,0:T(8,128)} %multiply_add_fusion) | data formatting | bytes 12582912 | tf_op jit(solution)/shard_map/add | solution.py:81
  (66 shorter events, 49.9 us)
Async XLA Ops:
  6.5 3.2 copy-start
  6.5 74.4 %all-reduce.3.cloned.1.call-start = ((), (), s32[]{:S(2)}) async-start(), calls=%async_computation | async-start | bytes 196608 | tf_op jit(solution)/shard_map/psum | solution.py:73
  10.8 6.6 %copy-start.3 = (s32[4,4]{1,0:T(4,128)S(1)}, s32[4,4]{1,0:T(4,128)}, u32[]{:S(2)}) copy-start(s32[4,4]{1,0:T(4,128)} %param.10) | copy-start | bytes 196
  12.3 70.1 %collective-permute-start = (bf16[16,128,384]{2,1,0:T(8,128)(2,1)}, bf16[16,128,384]{2,1,0:T(8,128)(2,1)}, u32[]{:S(2)}, u32[]{:S(2)}) collective-permute-start(bf16[16,128,384]{2,1,0:T(8,128)(2,1)} %bitcast.2), channel_id=1, source_target_pairs={{8,0},{16,8},{24,16},{0,24},{9,1},{17,9},{25,17},{1,25},{10,2},{18... | collective-permute-start | bytes 4718600 | tf_op jit(solution)/shard_map/ppermute | solution.py:12
  18.8 7.5 %copy-start.2 = (s32[4,8]{1,0:T(4,128)S(1)}, s32[4,8]{1,0:T(4,128)}, u32[]{:S(2)}) copy-start(s32[4,8]{1,0:T(4,128)} %param.11) | copy-start | bytes 388
  23.5 64.4 %collective-permute-start.1 = (bf16[16,128,384]{2,1,0:T(8,128)(2,1)}, bf16[16,128,384]{2,1,0:T(8,128)(2,1)}, u32[]{:S(2)}, u32[]{:S(2)}) collective-permute-start(bf16[16,128,384]{2,1,0:T(8,128)(2,1)} %broadcast_select_fusion.1), channel_id=1, source_target_pairs={{24,0},{0,8},{8,16},{16,24},{25,1},{1,9},{9,17},{17,25},{26,2},{2,... | collective-permute-start | bytes 4718600 | tf_op jit(solution)/shard_map/ppermute | solution.py:12
  27.3 276.3 %all-reduce.5.cloned.1.call-start = ((), (), s32[]{:S(2)}) async-start(), calls=%async_computation.1 | async-start | bytes 196608 | tf_op jit(solution)/shard_map/psum | solution.py:73
  27.4 53.5 %copy-start.1 = (f32[1,128,128]{2,1,0:T(8,128)S(1)}, f32[1,128,128]{2,1,0:T(8,128)}, u32[]{:S(2)}) copy-start(f32[1,128,128]{2,1,0:T(8,128)} %param.12) | copy-start | bytes 196612
  87.9 6.2 %slice-start = ((s8[6291456]{0:T(1024)(128)(4,1)}), s8[4194304]{0:T(1024)(128)(4,1)S(1)}, s32[]{:S(2)}) async-start(s8[6291456]{0:T(1024)(128)(4,1)} %bitcast.78), calls=%async_computation.2 | async-start | bytes 8388608
  90.4 3.7 slice-start.1
  241.6 70.7 %collective-permute-start.2 = (bf16[16,128,384]{1,2,0:T(8,128)(2,1)}, bf16[16,128,384]{1,2,0:T(8,128)(2,1)}, u32[]{:S(2)}, u32[]{:S(2)}) collective-permute-start(bf16[16,128,384]{1,2,0:T(8,128)(2,1)} %bitcast.16), channel_id=1, source_target_pairs={{8,0},{16,8},{24,16},{0,24},{9,1},{17,9},{25,17},{1,25},{10,2},{18... | collective-permute-start | bytes 4718600 | tf_op jit(solution)/shard_map/ppermute | solution.py:12
  246.2 74.4 %collective-permute-start.3 = (bf16[16,128,384]{1,2,0:T(8,128)(2,1)}, bf16[16,128,384]{1,2,0:T(8,128)(2,1)}, u32[]{:S(2)}, u32[]{:S(2)}) collective-permute-start(bf16[16,128,384]{1,2,0:T(8,128)(2,1)} %broadcast_select_fusion), channel_id=1, source_target_pairs={{24,0},{0,8},{8,16},{16,24},{25,1},{1,9},{9,17},{17,25},{26,2},{2,... | collective-permute-start | bytes 4718600 | tf_op jit(solution)/shard_map/ppermute | solution.py:12
Sparse Core Ops, SparseCore 0:
  27.4 53.4 all-reduce.2
  254.0 49.6 all-reduce.4
